TPU v7x, 32 devices: a whole 2x2x4 slice. The times are simulated.
32 devices in a mesh: row: 4 (over y, core), col: 8 (over z, x).
Axes of the slice: x: 2, y: 2, z: 4, core: 2. Of those that a mesh axis runs over, the one named last changes fastest.
Arguments:
- kernel: float32 [4, 4, 256, 2, 8, 256], P(None, 'row', None, None, 'col'), may hold values from -40 to 40, as said below
Outputs:
- trailing: float32 [4, 4, 256, 2, 8, 256], P(None, 'row', None, None, 'col')
- panels: float32 [4, 4, 256, 3, 256], P(None, 'row')
Inputs may be any that keep to these rules, and one draw needn't show every extreme that they name: kernel is symmetric and positive definite with smallest eigenvalue at least 1.
All inputs are finite; a program needn't handle non-finite values.
Results may differ from a plain program's by a relative error of at most 0.0003.
Values sent between devices are 32-bit elements; how exact they have to be, the bound alone decides.
A program may use at most 128 MiB of HBM per device.

v0:
```python
import jax
import jax.numpy as jnp
from jax import lax
from jax.sharding import PartitionSpec as P

STEPS = 3


def broadcast(value, axis, source):
    kept = jnp.where(lax.axis_index(axis) == source, value, 0).astype(value.dtype)
    return lax.psum(kept, axis)


def shards(kernel):
    row_tiles, _, tile_size, col_tiles, _, _ = kernel.shape
    row_count = lax.axis_size("row")
    col_count = lax.axis_size("col")
    row_index = lax.axis_index("row")
    col_index = lax.axis_index("col")
    stride = col_count // row_count
    working = kernel.reshape(row_tiles, tile_size, col_tiles, tile_size)
    identity = jnp.eye(tile_size, dtype=jnp.float32)
    tile_rows = jnp.arange(row_tiles) * row_count + row_index
    tile_cols = jnp.arange(col_tiles) * col_count + col_index
    collected = []
    for panel_step in range(STEPS):
        local_row = panel_step // row_count
        local_col = panel_step // col_count
        column_slab = working[:, :, local_col, :]
        diagonal = broadcast(column_slab[local_row], "row", panel_step % row_count)
        factor = jnp.linalg.cholesky(diagonal)
        inverse = lax.linalg.triangular_solve(factor, identity, left_side=True, lower=True)
        panel = jnp.einsum("art,st->ars", column_slab, inverse, precision=lax.Precision.HIGHEST)
        panel = jnp.where((tile_rows >= panel_step)[:, None, None], panel, jnp.float32(0.0))
        my_panel = broadcast(panel, "col", panel_step % col_count)
        collected.append(my_panel)
        selected = lax.dynamic_index_in_dim(
            my_panel.reshape(col_tiles, stride, tile_size, tile_size),
            col_index // row_count,
            1,
            keepdims=False,
        )
        gathered = lax.all_gather(selected, "row", axis=0, tiled=True)
        col_panel = lax.dynamic_index_in_dim(
            gathered.reshape(row_count, col_tiles, tile_size, tile_size),
            col_index % row_count,
            0,
            keepdims=False,
        )
        row_terms = jnp.where((tile_rows > panel_step)[:, None, None], my_panel, jnp.float32(0.0))
        col_terms = jnp.where((tile_cols > panel_step)[:, None, None], col_panel, jnp.float32(0.0))
        correction = jnp.einsum(
            "art,cst->arcs", row_terms, col_terms, precision=lax.Precision.HIGHEST
        )
        keep_mask = (tile_rows > panel_step)[:, None, None, None] & (tile_cols > panel_step)[
            None, None, :, None
        ]
        working = jnp.where(keep_mask, working - correction, jnp.float32(0.0))
    trailing = working.reshape(kernel.shape)
    panels = jnp.stack(collected, axis=2).reshape(row_tiles, 1, tile_size, STEPS, tile_size)
    return (trailing, panels)


def solution(mesh):
    in_specs = (P(None, "row", None, None, "col", None),)
    out_specs = (P(None, "row", None, None, "col", None), P(None, "row", None, None, None))
    return jax.shard_map(shards, mesh=mesh, in_specs=in_specs, out_specs=out_specs, check_vma=False)
```

profile of v0, /device:TPU:28, one launch (start us, length us, event | category | flops | bytes accessed | tf_op | source)
XLA Modules:
  0.0 666.0 jit_solution(3093933253821480764)
XLA Ops:
  7.2 4.6 copy.23
  12.7 32.2 %all-reduce.8.cloned.1.call-done = f32[256,256]{0,1:T(8,128)} async-done(((f32[256,256]{0,1:T(8,128)}), f32[256,256]{0,1:T(8,128)}) %all-reduce.8.cloned.1.call-update) | async-done | bytes 262160 | tf_op jit(solution)/shard_map/psum | solution.py:11
  46.9 11.7 %cholesky.172 = f32[128,128]{1,0:T(8,128)S(1)} custom-call(f32[128,128]{1,0:T(8,128)S(1)} %cholesky.270), custom_call_target="Cholesky" | custom-call | tf_op jit(solution)/shard_map/jit(cholesky)/cholesky | solution.py:31
  58.7 9.8 %custom-call.15 = f32[1,128,128]{1,2,0:T(8,128)S(1)} custom-call(f32[1,128,128]{2,1,0:T(8,128)S(1)} %get-tuple-element.72), custom_call_target="InvertDiagBlocksLowerTriangular" | custom-call | tf_op jit(solution)/shard_map/jit(cholesky)/cholesky | solution.py:31
  69.0 11.7 %cholesky.189 = f32[128,128]{1,0:T(8,128)S(1)} custom-call(f32[128,128]{1,0:T(8,128)S(1)} %convolution_subtract_fusion.5), custom_call_target="Cholesky" | custom-call | tf_op jit(solution)/shard_map/jit(cholesky)/cholesky | solution.py:31
  82.9 4.3 while.6
  83.8 1.4 bitcast_dynamic-update-slice_fusion.6
  85.8 1.4 bitcast_dynamic-update-slice_fusion.6
  87.3 19.7 %custom-call.16 = f32[2,128,128]{1,2,0:T(8,128)S(1)} custom-call(f32[2,128,128]{2,1,0:T(8,128)S(1)} %get-tuple-element.24), custom_call_target="InvertDiagBlocksLowerTriangular" | custom-call | tf_op jit(solution)/shard_map/triangular_solve/custom-call.0 | solution.py:32
  107.9 2.0 fusion.3
  110.0 78.2 %all-reduce.10.cloned.1.call-done = f32[4,256,256]{1,2,0:T(8,128)} async-done(((f32[4,256,256]{1,2,0:T(8,128)}), f32[4,256,256]{1,2,0:T(8,128)}) %all-reduce.10.cloned.1.call-update) | async-done | bytes 1048592 | tf_op jit(solution)/shard_map/psum | solution.py:11
  188.2 2.0 constant_dynamic-slice_fusion.5
  190.1 2.0 copy.60
  192.4 22.4 %all-gather.7.cloned.1.call-done = f32[8,1,256,256]{3,2,1,0:T(8,128)} async-done(((f32[2,1,256,256]{3,2,1,0:T(8,128)}), f32[8,1,256,256]{3,2,1,0:T(8,128)}) %all-gather.7.cloned.1.call-update) | async-done | bytes 2097168 | tf_op jit(solution)/shard_map/all_gather | solution.py:43
  214.8 3.2 subtract_select_fusion.1
  218.0 1.3 copy-done
  220.4 32.0 %all-reduce.12.cloned.1.call-done = f32[256,256]{0,1:T(8,128)} async-done(((f32[256,256]{0,1:T(8,128)}), f32[256,256]{0,1:T(8,128)}) %all-reduce.12.cloned.1.call-update) | async-done | bytes 262160 | tf_op jit(solution)/shard_map/psum | solution.py:11
  255.1 11.7 %cholesky.206 = f32[128,128]{1,0:T(8,128)S(1)} custom-call(f32[128,128]{1,0:T(8,128)S(1)} %cholesky.273), custom_call_target="Cholesky" | custom-call | tf_op jit(solution)/shard_map/jit(cholesky)/cholesky | solution.py:31
  267.5 10.4 %custom-call.17 = f32[1,128,128]{1,2,0:T(8,128)} custom-call(f32[1,128,128]{2,1,0:T(8,128)S(1)} %get-tuple-element.68), custom_call_target="InvertDiagBlocksLowerTriangular" | custom-call | tf_op jit(solution)/shard_map/jit(cholesky)/cholesky | solution.py:31
  278.7 1.7 constant_dynamic-update-slice_fusion.1
  281.5 11.7 %cholesky.223 = f32[128,128]{1,0:T(8,128)S(1)} custom-call(f32[128,128]{1,0:T(8,128)S(1)} %convolution_subtract_fusion.4), custom_call_target="Cholesky" | custom-call | tf_op jit(solution)/shard_map/jit(cholesky)/cholesky | solution.py:31
  296.6 6.3 while.7
  297.7 2.2 bitcast_dynamic-update-slice_fusion.7
  300.7 2.2 bitcast_dynamic-update-slice_fusion.7
  303.5 20.5 %custom-call.18 = f32[2,128,128]{1,2,0:T(8,128)S(1)} custom-call(f32[2,128,128]{2,1,0:T(8,128)} %copy-done.7), custom_call_target="InvertDiagBlocksLowerTriangular" | custom-call | tf_op jit(solution)/shard_map/triangular_solve/custom-call.0 | solution.py:32
  325.8 2.1 fusion.1
  327.9 78.2 %all-reduce.14.cloned.1.call-done = f32[4,256,256]{1,2,0:T(8,128)} async-done(((f32[4,256,256]{1,2,0:T(8,128)}), f32[4,256,256]{1,2,0:T(8,128)}) %all-reduce.14.cloned.1.call-update) | async-done | bytes 1048592 | tf_op jit(solution)/shard_map/psum | solution.py:11
  408.4 22.5 %all-gather.9.cloned.1.call-done = f32[8,1,256,256]{3,2,1,0:T(8,128)} async-done(((f32[2,1,256,256]{3,2,1,0:T(8,128)}), f32[8,1,256,256]{3,2,1,0:T(8,128)}) %all-gather.9.cloned.1.call-update) | async-done | bytes 2097168 | tf_op jit(solution)/shard_map/all_gather | solution.py:43
  430.8 4.2 subtract_select_fusion
  436.0 32.0 %all-reduce.16.cloned.1.call-done = f32[256,256]{0,1:T(8,128)} async-done(((f32[256,256]{0,1:T(8,128)}), f32[256,256]{0,1:T(8,128)}) %all-reduce.16.cloned.1.call-update) | async-done | bytes 262160 | tf_op jit(solution)/shard_map/psum | solution.py:11
  468.0 1.8 copy.35
  471.6 11.7 %cholesky.240 = f32[128,128]{1,0:T(8,128)S(1)} custom-call(f32[128,128]{1,0:T(8,128)S(1)} %cholesky.276), custom_call_target="Cholesky" | custom-call | tf_op jit(solution)/shard_map/jit(cholesky)/cholesky | solution.py:31
  484.0 10.4 %custom-call.19 = f32[1,128,128]{1,2,0:T(8,128)} custom-call(f32[1,128,128]{2,1,0:T(8,128)S(1)} %get-tuple-element.64), custom_call_target="InvertDiagBlocksLowerTriangular" | custom-call | tf_op jit(solution)/shard_map/jit(cholesky)/cholesky | solution.py:31
  495.2 1.7 constant_dynamic-update-slice_fusion
  498.0 11.7 %cholesky.257 = f32[128,128]{1,0:T(8,128)S(1)} custom-call(f32[128,128]{1,0:T(8,128)S(1)} %convolution_subtract_fusion.3), custom_call_target="Cholesky" | custom-call | tf_op jit(solution)/shard_map/jit(cholesky)/cholesky | solution.py:31
  513.0 5.9 while.8
  513.8 2.3 bitcast_dynamic-update-slice_fusion.8
  516.7 2.2 bitcast_dynamic-update-slice_fusion.8
  519.6 20.5 %custom-call.20 = f32[2,128,128]{1,2,0:T(8,128)S(1)} custom-call(f32[2,128,128]{2,1,0:T(8,128)} %copy-done.6), custom_call_target="InvertDiagBlocksLowerTriangular" | custom-call | tf_op jit(solution)/shard_map/triangular_solve/custom-call.0 | solution.py:32
  541.8 2.1 fusion
  543.9 78.2 %all-reduce.18.cloned.1.call-done = f32[4,256,256]{1,2,0:T(8,128)} async-done(((f32[4,256,256]{1,2,0:T(8,128)}), f32[4,256,256]{1,2,0:T(8,128)}) %all-reduce.18.cloned.1.call-update) | async-done | bytes 1048592 | tf_op jit(solution)/shard_map/psum | solution.py:11
  622.2 1.9 constant_dynamic-slice_fusion.3
  624.0 2.0 copy.62
  626.2 3.4 maximum_bitcast_fusion
  629.6 3.6 copy.42
  633.2 15.5 %all-gather.11.cloned.1.call-done = f32[8,1,256,256]{3,2,1,0:T(8,128)} async-done(((f32[2,1,256,256]{3,2,1,0:T(8,128)}), f32[8,1,256,256]{3,2,1,0:T(8,128)}) %all-gather.11.cloned.1.call-update) | async-done | bytes 2097168 | tf_op jit(solution)/shard_map/all_gather | solution.py:43
  648.7 4.5 select_bitcast_fusion
  653.2 6.0 copy.41
  (106 shorter events, 32.0 us)
Async XLA Ops:
  7.2 37.7 %all-reduce.8.cloned.1.call-start = ((), (), s32[]{:S(2)}) async-start(), calls=%async_computation | async-start | bytes 524288 | tf_op jit(solution)/shard_map/psum | solution.py:11
  12.5 175.6 %all-reduce.10.cloned.1.call-start = ((), (), s32[]{:S(2)}) async-start(), calls=%async_computation.1 | async-start | bytes 2097152 | tf_op jit(solution)/shard_map/psum | solution.py:11
  109.9 104.9 %all-gather.7.cloned.1.call-start = ((), (), s32[]{:S(2)}) async-start(), calls=%async_computation.6 | async-start | bytes 2621440 | tf_op jit(solution)/shard_map/all_gather | solution.py:43
  188.2 26.6 %copy-start.2 = (f32[4,256,256]{1,2,0:T(8,128)S(1)}, f32[4,256,256]{1,2,0:T(8,128)}, u32[]{:S(2)}) copy-start(f32[4,256,256]{1,2,0:T(8,128)} %all-reduce.10.cloned.1.call-done) | copy-start | bytes 3145732
  192.2 60.2 %all-reduce.12.cloned.1.call-start = ((), (), s32[]{:S(2)}) async-start(), calls=%async_computation.2 | async-start | bytes 524288 | tf_op jit(solution)/shard_map/psum | solution.py:11
  218.0 1.3 copy-start
  220.1 186.0 %all-reduce.14.cloned.1.call-start = ((), (), s32[]{:S(2)}) async-start(), calls=%async_computation.3 | async-start | bytes 2097152 | tf_op jit(solution)/shard_map/psum | solution.py:11
  254.4 0.7 copy-start.4
  255.1 70.6 %copy-start.1 = (f32[4,256,2,256]{1,3,2,0:T(8,128)S(1)}, f32[4,256,2,256]{1,3,2,0:T(8,128)}, u32[]{:S(2)}) copy-start(f32[4,256,2,256]{1,3,2,0:T(8,128)} %copy-done) | copy-start | bytes 6291460
  302.9 0.6 copy-start.7
  327.8 103.0 %all-gather.9.cloned.1.call-start = ((), (), s32[]{:S(2)}) async-start(), calls=%async_computation.7 | async-start | bytes 2621440 | tf_op jit(solution)/shard_map/all_gather | solution.py:43
  408.2 59.8 %all-reduce.16.cloned.1.call-start = ((), (), s32[]{:S(2)}) async-start(), calls=%async_computation.4 | async-start | bytes 524288 | tf_op jit(solution)/shard_map/psum | solution.py:11
  435.8 186.4 %all-reduce.18.cloned.1.call-start = ((), (), s32[]{:S(2)}) async-start(), calls=%async_computation.5 | async-start | bytes 2097152 | tf_op jit(solution)/shard_map/psum | solution.py:11
  470.9 0.7 copy-start.5
  518.9 0.7 copy-start.6
  543.9 104.8 %all-gather.11.cloned.1.call-start = ((), (), s32[]{:S(2)}) async-start(), calls=%async_computation.8 | async-start | bytes 2621440 | tf_op jit(solution)/shard_map/all_gather | solution.py:43
  629.6 19.1 %copy-start.3 = (f32[4,256,256]{1,2,0:T(8,128)S(1)}, f32[4,256,256]{1,2,0:T(8,128)}, u32[]{:S(2)}) copy-start(f32[4,256,256]{1,2,0:T(8,128)} %all-reduce.18.cloned.1.call-done) | copy-start | bytes 3145732
Sparse Core Ops, SparseCore 0:
  12.7 32.1 all-reduce.7
  110.0 78.1 all-reduce.9
  192.3 22.4 all-gather.6
  220.2 32.1 all-reduce.11
  328.0 78.0 all-reduce.13
  408.3 22.4 all-gather.8
  435.9 32.1 all-reduce.15
  544.0 78.1 all-reduce.17
  626.2 22.4 all-gather.10
where the time goes:
time: 678 us; the launch traced here: 666 us
  waiting for transfers between devices  391 us (58%)
  other arithmetic  177 us (26%)
  local copies, waits for them, and re-layouts  49.2 us (7%)
  matrix products  28.4 us (4%)
  between operations  18.4 us (3%)
    psum x6, waiting for transfers between devices, broadcast(): return lax.psum(kept, axis)  331 us
    another operation x20, other arithmetic, shards(): factor = jnp.linalg.cholesky(diagonal)  106 us
    another operation x7, other arithmetic, shards(): lax.linalg.triangular_solve(factor, identity, left_side=True, lower=True)  62.2 us
    all_gather x3, waiting for transfers between devices, shards(): gathered = lax.all_gather(selected, 'row', axis=0, tiled=True)  60.4 us
    unnamed x22, local copies, waits for them, and re-layouts  23.3 us
    another operation x22, local copies, waits for them, and re-layouts, shards(): lax.linalg.triangular_solve(factor, identity, left_side=True, lower=True)  15.6 us
  transfers between devices with their start and end apart: 9, of which 9 were waited for; matrix products, arithmetic and copies ran while one was open for 1% of the time, Pallas kernels for 0%

commit v1 on v0

v1 whole, which is shorter than its diff:
```python
import functools

import jax
import jax.numpy as jnp
from jax import lax
from jax.experimental import pallas as pl
from jax.experimental.pallas import tpu as pltpu
from jax.sharding import PartitionSpec as P

STEPS = 3
PANEL = 16
MESH = pl.DeviceIdType.MESH
F32 = jnp.float32
BF16 = jnp.bfloat16
LOWER = [(i, j) for j in range(STEPS) for i in range(j, STEPS)]
SLOT = {ij: n for n, ij in enumerate(LOWER)}


def split_col(cols):
    width = 1
    while width * width * 4 <= cols:
        width *= 2
    return width, cols // width


def exchange_kernel(R, C, x_ref, ld_ref, rs_ref, cs_ref, send_sem, local_sem, ld_sem, ldx_sem, rs_sem, cs_sem):
    A, B, T, _ = x_ref.shape
    X, Z = split_col(C)
    r, c = lax.axis_index("row"), lax.axis_index("col")
    z, x = lax.div(c, X), lax.rem(c, X)
    chunk = T // R
    pending = []
    counts = {"send": 0, "local": 0}

    def send(cond, src, dst, sem, dev):
        n = counts["send"]
        counts["send"] += 1
        copy = pltpu.make_async_remote_copy(
            src_ref=src, dst_ref=dst, send_sem=send_sem.at[n], recv_sem=sem, device_id=dev, device_id_type=MESH
        )
        pl.when(cond)(copy.start)
        pending.append((cond, copy.wait_send))

    def local(cond, src, dst):
        n = counts["local"]
        counts["local"] += 1
        copy = pltpu.make_async_copy(src, dst, local_sem.at[n])
        pl.when(cond)(copy.start)
        return copy.wait

    def wait_recv(cond, dst, sem):
        copy = pltpu.make_async_remote_copy(
            src_ref=dst, dst_ref=dst, send_sem=send_sem.at[0], recv_sem=sem,
            device_id=(lax.rem(r + 1, R), c), device_id_type=MESH,
        )
        pl.when(cond)(copy.wait_recv)

    def rows_of(n, q):
        return ld_ref.at[n, pl.ds(pl.multiple_of(q * chunk, chunk), chunk), :]

    def part(ref, q):
        return ref.at[pl.ds(pl.multiple_of(q * chunk, chunk), chunk), :]

    ld_local = []
    for n, (i, j) in enumerate(LOWER):
        src = x_ref.at[i // R, j // C]
        owner = (r == i % R) & (c == j % C)
        for step in range(1, R):
            q = lax.rem(r + step, R)
            send(owner, part(src, q), rows_of(n, q), ld_sem.at[n], (q, c))
        ld_local.append(local(owner, part(src, r), rows_of(n, r)))
    rs_local = {}
    for k in range(STEPS):
        for a in range(A):
            rs_local[k, a] = local(c == k % C, x_ref.at[a, k // C], rs_ref.at[k, a])
    cs_local = {}
    for k in range(STEPS):
        for b in range(B):
            src, dst = x_ref.at[k // R, b], cs_ref.at[k, b]
            for step in range(1, R):
                send(r == k % R, src, dst, cs_sem.at[k, b], (lax.rem(r + step, R), c))
            cs_local[k, b] = local(r == k % R, src, dst)

    def spread(slot, sem, source, lane):
        zs, xs = divmod(source, X)
        if lane != xs:
            send(c == source, slot, slot, sem, (r, zs * X + lane))
        on = x == lane
        send(on & (z >= zs) & (z + 1 < Z), slot, slot, sem, (r, lax.rem(c + X, C)))
        send(on & (z <= zs) & (z > 0), slot, slot, sem, (r, lax.rem(c + C - X, C)))
        for other in range(X):
            if other != lane:
                cond = on & (z != zs) if other == xs else on
                send(cond, slot, slot, sem, (r, z * X + other))

    for n, (i, j) in enumerate(LOWER):
        owner = (r == i % R) & (c == j % C)
        slot = rows_of(n, r)
        pl.when(owner)(ld_local[n])
        wait_recv(jnp.logical_not(owner), slot, ld_sem.at[n])
        spread(slot, ld_sem.at[n], j % C, n % X)
        for step in range(1, R):
            q = lax.rem(r + step, R)
            send(r >= 0, slot, slot, ldx_sem.at[n, step - 1], (q, c))
    for a in range(A):
        for k in range(STEPS):
            slot = rs_ref.at[k, a]
            pl.when(c == k % C)(rs_local[k, a])
            wait_recv(c != k % C, slot, rs_sem.at[k, a])
            spread(slot, rs_sem.at[k, a], k % C, k % X if k < X else a % X)
    for n in range(len(LOWER)):
        for step in range(1, R):
            q = lax.rem(r + R - step, R)
            wait_recv(r >= 0, rows_of(n, q), ldx_sem.at[n, step - 1])
    for k in range(STEPS):
        for b in range(B):
            pl.when(r == k % R)(cs_local[k, b])
            wait_recv(r != k % R, cs_ref.at[k, b], cs_sem.at[k, b])
    for cond, wait in pending:
        pl.when(cond)(wait)


def exchange(tiles, R, C):
    A, B, T, _ = tiles.shape
    X, _ = split_col(C)
    n = len(LOWER)
    vmem = pl.BlockSpec(memory_space=pltpu.VMEM)
    sends = n * (R - 1) * 2 + STEPS * B * (R - 1) + (n + STEPS * A) * (X + 2)
    locals_ = n + STEPS * A + STEPS * B
    dma = pltpu.SemaphoreType.DMA
    return pl.pallas_call(
        functools.partial(exchange_kernel, R, C),
        name="exchange",
        out_shape=(
            jax.ShapeDtypeStruct((n, T, T), F32),
            jax.ShapeDtypeStruct((STEPS, A, T, T), F32),
            jax.ShapeDtypeStruct((STEPS, B, T, T), F32),
        ),
        in_specs=[vmem],
        out_specs=(vmem, vmem, vmem),
        scratch_shapes=[dma((sends,)), dma((locals_,)), dma((n,)), dma((n, R - 1)), dma((STEPS, A)), dma((STEPS, B))],
        compiler_params=pltpu.CompilerParams(has_side_effects=True, vmem_limit_bytes=56 * 2**20),
    )(tiles)


def dot_nt(p, q):
    return lax.dot_general(p, q, (((1,), (1,)), ((), ())), precision=lax.Precision.HIGHEST, preferred_element_type=F32)


def dot_nn(p, q):
    return lax.dot_general(p, q, (((1,), (0,)), ((), ())), precision=lax.Precision.HIGHEST, preferred_element_type=F32)


def invert_factor(w_ref):
    T = w_ref.shape[0]
    b = PANEL
    lane = lax.broadcasted_iota(jnp.int32, (b, T), 1)
    sub = lax.broadcasted_iota(jnp.int32, (b, T), 0)
    row = lax.broadcasted_iota(jnp.int32, (T, T), 0)
    col = lax.broadcasted_iota(jnp.int32, (T, T), 1)

    def body(p, carry):
        base = pl.multiple_of(p * b, b)
        R = w_ref[pl.ds(base, b), :]
        E = jnp.where(lane == base + sub, F32(1.0), F32(0.0))
        cols = []
        for j in range(b):
            picked = jnp.sum(jnp.where(lane == base + j, R, F32(0.0)), axis=1, keepdims=True)
            cols.append(jnp.broadcast_to(picked, (b, T)))
        diag = jnp.ones((b, T), F32)
        for j in range(b):
            d = jnp.broadcast_to(cols[j][j : j + 1, :], (b, T))
            diag = jnp.where(sub == j, d, diag)
            if j == b - 1:
                break
            w = jnp.where(sub > j, cols[j] * (F32(1.0) / d), F32(0.0))
            for i in range(j + 1, b):
                cols[i] = cols[i] - w * cols[i][j : j + 1, :]
            R = R - w * R[j : j + 1, :]
            E = E - w * E[j : j + 1, :]
        scale = lax.rsqrt(diag)
        R = R * scale
        E = E * scale
        V = jnp.where((lane >= base) & (lane < base + b), E, R)
        coef = jnp.where(lane >= base + b, R, F32(0.0))
        update = lax.dot_general(
            coef, V, (((0,), (0,)), ((), ())), precision=lax.Precision.HIGHEST, preferred_element_type=F32
        )
        drop = (row >= base + b) & (col >= base) & (col < base + b)
        w_ref[...] = jnp.where(drop, F32(0.0), w_ref[...]) - update
        w_ref[pl.ds(base, b), :] = V
        return carry

    lax.fori_loop(0, T // b, body, 0)
    w_ref[...] = jnp.where(row >= col, w_ref[...], F32(0.0))


def factor_kernel(ld_ref, m_ref, w_ref):
    for n in range(len(LOWER)):
        w_ref[n] = ld_ref[n]
    for k in range(STEPS):
        invert_factor(w_ref.at[SLOT[k, k]])
        inv = w_ref[SLOT[k, k]]
        for i in range(k + 1, STEPS):
            w_ref[SLOT[i, k]] = dot_nt(w_ref[SLOT[i, k]], inv)
        for j in range(k + 1, STEPS):
            for i in range(j, STEPS):
                w_ref[SLOT[i, j]] = w_ref[SLOT[i, j]] - dot_nt(w_ref[SLOT[i, k]], w_ref[SLOT[j, k]])
    for k in range(STEPS):
        m_ref[SLOT[k, k]] = w_ref[SLOT[k, k]]
        for i in range(k + 1, STEPS):
            total = dot_nn(w_ref[SLOT[i, k]], m_ref[SLOT[k, k]])
            for j in range(k + 1, i):
                total = total + dot_nn(w_ref[SLOT[i, j]], m_ref[SLOT[j, k]])
            m_ref[SLOT[i, k]] = -dot_nn(w_ref[SLOT[i, i]], total)


def factor(lead):
    vmem = pl.BlockSpec(memory_space=pltpu.VMEM)
    return pl.pallas_call(
        factor_kernel,
        name="factor",
        out_shape=jax.ShapeDtypeStruct(lead.shape, F32),
        in_specs=[vmem],
        out_specs=vmem,
        scratch_shapes=[pltpu.VMEM(lead.shape, F32)],
        compiler_params=pltpu.CompilerParams(vmem_limit_bytes=56 * 2**20),
    )(lead)


def halves(value):
    high = value.astype(BF16)
    return high, (value - high.astype(F32)).astype(BF16)


def dot3(p, q, dims):
    d = functools.partial(lax.dot_general, dimension_numbers=(dims, ((), ())), preferred_element_type=F32)
    return d(p[0], q[0]) + (d(p[0], q[1]) + d(p[1], q[0]))


NT = ((1,), (1,))
NN = ((1,), (0,))


def finish_kernel(R, C, x_ref, m_ref, rs_ref, cs_ref, t_ref, p_ref, mh_ref, ml_ref, qh_ref, ql_ref):
    A, B, T, _ = x_ref.shape
    r, c = lax.axis_index("row"), lax.axis_index("col")
    for n in range(len(LOWER)):
        mh_ref[n], ml_ref[n] = halves(m_ref[n])
    for b in range(B):
        terms = [halves(cs_ref[j, b]) for j in range(STEPS)]
        for k in range(STEPS):
            total = None
            for j in range(k + 1):
                n = SLOT[k, j]
                term = dot3((mh_ref[n], ml_ref[n]), terms[j], NN)
                total = term if total is None else total + term
            qh_ref[k, b], ql_ref[k, b] = halves(total)

    def body(a, carry):
        tile_row = a * R + r
        terms = [halves(rs_ref[j, a]) for j in range(STEPS)]
        panel = []
        for k in range(STEPS):
            total = None
            for j in range(k + 1):
                n = SLOT[k, j]
                term = dot3(terms[j], (mh_ref[n], ml_ref[n]), NT)
                total = term if total is None else total + term
            p_ref[a, k] = jnp.where(tile_row >= k, total, F32(0.0))
            panel.append(halves(total))
        for b in range(B):
            total = x_ref[a, b]
            for k in range(STEPS):
                total = total - dot3(panel[k], (qh_ref[k, b], ql_ref[k, b]), NN)
            keep = (tile_row >= STEPS) & (b * C + c >= STEPS)
            t_ref[a, :, b * T : (b + 1) * T] = jnp.where(keep, total, F32(0.0))
        return carry

    lax.fori_loop(0, A, body, 0)


def finish(tiles, m, rs, cs, R, C):
    A, B, T, _ = tiles.shape
    vmem = pl.BlockSpec(memory_space=pltpu.VMEM)
    n = len(LOWER)
    return pl.pallas_call(
        functools.partial(finish_kernel, R, C),
        name="finish",
        out_shape=(jax.ShapeDtypeStruct((A, T, B * T), F32), jax.ShapeDtypeStruct((A, STEPS, T, T), F32)),
        in_specs=[vmem] * 4,
        out_specs=(vmem, vmem),
        scratch_shapes=[
            pltpu.VMEM((n, T, T), BF16),
            pltpu.VMEM((n, T, T), BF16),
            pltpu.VMEM((STEPS, B, T, T), BF16),
            pltpu.VMEM((STEPS, B, T, T), BF16),
        ],
        compiler_params=pltpu.CompilerParams(vmem_limit_bytes=56 * 2**20),
    )(tiles, m, rs, cs)


def shards(kernel):
    A, _, T, B, _, _ = kernel.shape
    R, C = lax.axis_size("row"), lax.axis_size("col")
    tiles = kernel.reshape(A, T, B, T).transpose(0, 2, 1, 3)
    ld, rs, cs = exchange(tiles, R, C)
    m = factor(ld)
    trailing, panels = finish(tiles, m, rs, cs, R, C)
    return trailing.reshape(kernel.shape), panels.transpose(0, 2, 1, 3).reshape(A, 1, T, STEPS, T)


def solution(mesh):
    in_specs = (P(None, "row", None, None, "col", None),)
    out_specs = (P(None, "row", None, None, "col", None), P(None, "row", None, None, None))
    return jax.shard_map(shards, mesh=mesh, in_specs=in_specs, out_specs=out_specs, check_vma=False)
```

time: 678 us -> 225 us (0.33); the launches traced: 666 us -> 225 us
  waiting for transfers between devices: 391 us -> 0 us
  Pallas kernels: 0 us -> 216 us
  other arithmetic: 177 us -> 0 us
  local copies, waits for them, and re-layouts: 49.2 us -> 7.81 us
  matrix products: 28.4 us -> 0 us
  between operations: 18.4 us -> 0.64 us
    psum x6 -> x0, waiting for transfers between devices: 331 us -> none  [broadcast(): return lax.psum(kept, axis)]
    pallas_call x0 -> x3, Pallas kernels: none -> 216 us  [the longest x1 163 us: exchange(): pl.pallas_call(functools.partial(exchange_kernel, R, C), name='exchange',...]
    another operation x27 -> x0, other arithmetic: 168 us -> none  [the longest x20 106 us: shards(): factor = jnp.linalg.cholesky(diagonal)]
    all_gather x3 -> x0, waiting for transfers between devices: 60.4 us -> none  [shards(): gathered = lax.all_gather(selected, 'row', axis=0, tiled=True)]
    unnamed x22 -> x1, local copies, waits for them, and re-layouts: 23.3 us -> 3.11 us
    dot_general x6 -> x0, matrix products: 18 us -> none  [the longest x3 11.9 us: shards(): jnp.einsum('art,cst->arcs', row_terms, col_terms, precision=lax.Precision...]
    another operation x28 -> x0, local copies, waits for them, and re-layouts: 17.1 us -> none  [the longest x22 15.6 us: shards(): lax.linalg.triangular_solve(factor, identity, left_side=True, lower=True)]
    another operation x15 -> x0, matrix products: 10.4 us -> none  [the longest x6 6.09 us: shards(): factor = jnp.linalg.cholesky(diagonal)]
  transfers between devices with their start and end apart: 9 -> 0, of which waited for: 9 -> 0; matrix products, arithmetic and copies ran while one was open for 1% -> 0% of each run, Pallas kernels for 0% -> 0%
where the time goes in v1:
time: 225 us
  Pallas kernels  216 us (96%)
  local copies, waits for them, and re-layouts  7.81 us (3%)
    pallas_call x1, Pallas kernels, exchange(): pl.pallas_call(functools.partial(exchange_kernel, R, C), name='exchange',...  163 us
    pallas_call x1, Pallas kernels, factor(): pl.pallas_call(factor_kernel, name='factor', out_shape=jax.ShapeDtypeStru...  40.4 us
    pallas_call x1, Pallas kernels, finish(): pl.pallas_call(functools.partial(finish_kernel, R, C), name='finish', out...  12.8 us
    reshape x1, local copies, waits for them, and re-layouts, shards(): trailing.reshape(kernel.shape)  4.7 us

profile of v1, /device:TPU:28, one launch (start us, length us, event | category | flops | bytes accessed | tf_op | source)
XLA Modules:
  0.0 224.6 jit_solution(3408054978488808423)
XLA Ops:
  0.6 3.1 %copy.7 = f32[4,1,256,2,1,256]{5,2,3,0,4,1:T(8,128)} copy(f32[4,1,256,2,1,256]{5,4,3,2,1,0:T(1,128)} %param.1) | data formatting | bytes 4194304 | tf_op args[0]
  3.7 162.9 %exchange.1 = (f32[6,256,256]{2,1,0:T(8,128)}, f32[3,4,256,256]{3,2,1,0:T(8,128)}, f32[3,2,256,256]{3,2,1,0:T(8,128)}) custom-call(f32[4,2,256,256]{3,2,1,0:T(8,128)} %bitcast.10), custom_call_target="tpu_custom_call" | custom-call | tf_op jit(solution)/shard_map/exchange/pallas_call | solution.py:131
  166.7 40.4 %factor.1.m_ref = f32[6,256,256]{2,1,0:T(8,128)} custom-call(f32[6,256,256]{2,1,0:T(8,128)} %get-tuple-element.7.ld_ref), custom_call_target="tpu_custom_call" | custom-call | tf_op jit(solution)/shard_map/factor/pallas_call | solution.py:220
  207.1 12.8 %finish.1 = (f32[4,256,512]{2,1,0:T(8,128)}, f32[4,3,256,256]{3,2,1,0:T(8,128)}) custom-call(f32[4,2,256,256]{3,2,1,0:T(8,128)} %bitcast.11, f32[6,256,256]{2,1,0:T(8,128)} %factor.1.m_ref, f32[3,4,256,256]{3,2,1,0:T(8,128)} %get-tuple-element.8.rs_ref, f32[3,2,256,256]{3,2,1,0:T(8,128)} %get-tuple-element.9.cs_ref), custom_call_target="tpu_custom_call" | custom-call | tf_op jit(solution)/shard_map/finish/pallas_call | solution.py:287
  219.9 4.7 %reshape.16 = f32[4,1,256,2,1,256]{5,4,3,2,1,0:T(1,128)} reshape(f32[4,256,512]{2,1,0:T(8,128)} %get-tuple-element.10) | data formatting | bytes 4194304 | tf_op jit(solution)/shard_map/reshape | solution.py:310

commit v2 on v1

v2 whole, which is shorter than its diff:
```python
import functools

import jax
import jax.numpy as jnp
from jax import lax
from jax.experimental import pallas as pl
from jax.experimental.pallas import tpu as pltpu
from jax.sharding import PartitionSpec as P

STEPS = 3
PANEL = 16
GROUPS = 4
SKEW = 2
MESH = pl.DeviceIdType.MESH
F32 = jnp.float32
BF16 = jnp.bfloat16
LOWER = [(i, j) for j in range(STEPS) for i in range(j, STEPS)]
SLOT = {ij: n for n, ij in enumerate(LOWER)}


def split_col(cols):
    width = 1
    while width * width * 4 <= cols:
        width *= 2
    return width, cols // width


def dot_nt(p, q):
    return lax.dot_general(p, q, (((1,), (1,)), ((), ())), precision=lax.Precision.HIGHEST, preferred_element_type=F32)


def dot_nn(p, q):
    return lax.dot_general(p, q, (((1,), (0,)), ((), ())), precision=lax.Precision.HIGHEST, preferred_element_type=F32)


def invert_factor(w_ref, between):
    T = w_ref.shape[0]
    b = PANEL
    lane = lax.broadcasted_iota(jnp.int32, (b, T), 1)
    sub = lax.broadcasted_iota(jnp.int32, (b, T), 0)
    row = lax.broadcasted_iota(jnp.int32, (T, T), 0)
    col = lax.broadcasted_iota(jnp.int32, (T, T), 1)

    def body(p, carry):
        base = pl.multiple_of(p * b, b)
        R = w_ref[pl.ds(base, b), :]
        E = jnp.where(lane == base + sub, F32(1.0), F32(0.0))
        cols = []
        for j in range(b):
            picked = jnp.sum(jnp.where(lane == base + j, R, F32(0.0)), axis=1, keepdims=True)
            cols.append(jnp.broadcast_to(picked, (b, T)))
        diag = jnp.ones((b, T), F32)
        for j in range(b):
            d = jnp.broadcast_to(cols[j][j : j + 1, :], (b, T))
            diag = jnp.where(sub == j, d, diag)
            if j == b - 1:
                break
            w = jnp.where(sub > j, cols[j] * (F32(1.0) / d), F32(0.0))
            for i in range(j + 1, b):
                cols[i] = cols[i] - w * cols[i][j : j + 1, :]
            R = R - w * R[j : j + 1, :]
            E = E - w * E[j : j + 1, :]
        scale = lax.rsqrt(diag)
        R = R * scale
        E = E * scale
        V = jnp.where((lane >= base) & (lane < base + b), E, R)
        coef = jnp.where(lane >= base + b, R, F32(0.0))
        update = lax.dot_general(
            coef, V, (((0,), (0,)), ((), ())), precision=lax.Precision.HIGHEST, preferred_element_type=F32
        )
        drop = (row >= base + b) & (col >= base) & (col < base + b)
        w_ref[...] = jnp.where(drop, F32(0.0), w_ref[...]) - update
        w_ref[pl.ds(base, b), :] = V
        return carry

    inner = T // b // GROUPS

    def group(g, carry):
        lax.fori_loop(g * inner, (g + 1) * inner, body, 0)
        between(g)
        return carry

    lax.fori_loop(0, GROUPS, group, 0)
    w_ref[...] = jnp.where(row >= col, w_ref[...], F32(0.0))


def lead_kernel(
    R, C, x_ref, m_ref, rs_ref, cs_ref, ld_ref, w_ref,
    send_sem, local_sem, ld_sem, ldx_sem, rs_sem, cs_sem, rs_send, rs_loc,
):
    A, B, T, _ = x_ref.shape
    X, Z = split_col(C)
    r, c = lax.axis_index("row"), lax.axis_index("col")
    z, x = lax.div(c, X), lax.rem(c, X)
    chunk = T // R
    items = A * STEPS
    pending = []
    counts = {"send": 0, "local": 0}

    def send(cond, src, dst, sem, dev):
        n = counts["send"]
        counts["send"] += 1
        copy = pltpu.make_async_remote_copy(
            src_ref=src, dst_ref=dst, send_sem=send_sem.at[n], recv_sem=sem, device_id=dev, device_id_type=MESH
        )
        pl.when(cond)(copy.start)
        pending.append((cond, copy.wait_send))

    def local(cond, src, dst):
        n = counts["local"]
        counts["local"] += 1
        copy = pltpu.make_async_copy(src, dst, local_sem.at[n])
        pl.when(cond)(copy.start)
        return copy.wait

    def wait_recv(cond, dst, sem):
        copy = pltpu.make_async_remote_copy(
            src_ref=dst, dst_ref=dst, send_sem=send_sem.at[0], recv_sem=sem,
            device_id=(lax.rem(r + 1, R), c), device_id_type=MESH,
        )
        pl.when(cond)(copy.wait_recv)

    def part(ref, q):
        return ref.at[pl.ds(pl.multiple_of(q * chunk, chunk), chunk), :]

    ld_local = []
    for n, (i, j) in enumerate(LOWER):
        src = x_ref.at[i // R, j // C]
        owner = (r == i % R) & (c == j % C)
        for step in range(1, R):
            q = lax.rem(r + step, R)
            send(owner, part(src, q), part(ld_ref.at[n], q), ld_sem.at[n], (q, c))
        ld_local.append(local(owner, part(src, r), part(ld_ref.at[n], r)))

    def item(m):
        k, a = lax.rem(m, STEPS), lax.div(m, STEPS)
        source = lax.rem(k, C)
        zs, xs = lax.div(source, X), lax.rem(source, X)
        lane = jnp.where(k < X, lax.rem(k, X), lax.rem(a, X))
        return k, a, source, zs, xs, lane

    def own_copy(m):
        k, a, source, _, _, _ = item(m)
        copy = pltpu.make_async_copy(x_ref.at[a, lax.div(k, C)], rs_ref.at[k, a], rs_loc.at[m])
        return c == source, copy

    def spread(m):
        k, a, source, zs, xs, lane = item(m)
        on = x == lane
        slot = rs_ref.at[k, a]

        def copy(n, dev):
            return pltpu.make_async_remote_copy(
                src_ref=slot, dst_ref=slot, send_sem=rs_send.at[m, n], recv_sem=rs_sem.at[m],
                device_id=dev, device_id_type=MESH,
            )

        yield (c == source) & (xs != lane), copy(0, (r, lax.rem(zs * X + lane, C)))
        yield on & (z >= zs) & (z + 1 < Z), copy(1, (r, lax.rem(c + X, C)))
        yield on & (z <= zs) & (z > 0), copy(2, (r, lax.rem(c + C - X, C)))
        for step in range(1, X):
            other = lax.rem(lane + step, X)
            yield on & jnp.logical_not((z == zs) & (other == xs)), copy(2 + step, (r, z * X + other))

    def start_own(m, carry):
        cond, copy = own_copy(m)
        pl.when(cond)(copy.start)
        return carry

    lax.fori_loop(0, items, start_own, 0)

    def lead_step(n, when):
        i, j = LOWER[n]
        owner = (r == i % R) & (c == j % C)
        slot = part(ld_ref.at[n], r)
        pl.when(owner & when)(ld_local[n])
        wait_recv(jnp.logical_not(owner) & when, slot, ld_sem.at[n])
        return slot

    def lead_swap(n, slot, when):
        for step in range(1, R):
            send(when, slot, slot, ldx_sem.at[n, step - 1], (lax.rem(r + step, R), c))

    for early in (True, False):
        for n, (i, j) in enumerate(LOWER):
            lane, source = n % X, j % C
            zs, xs = divmod(source, X)
            on = x == lane
            first = on | (c == source)
            when = first if early else jnp.logical_not(first)
            slot = lead_step(n, when)
            if early:
                if lane != xs:
                    send(c == source, slot, slot, ld_sem.at[n], (r, zs * X + lane))
                send(on & (z >= zs) & (z + 1 < Z), slot, slot, ld_sem.at[n], (r, lax.rem(c + X, C)))
                send(on & (z <= zs) & (z > 0), slot, slot, ld_sem.at[n], (r, lax.rem(c + C - X, C)))
                for other in range(X):
                    if other != lane:
                        cond = on & (z != zs) if other == xs else on
                        send(cond, slot, slot, ld_sem.at[n], (r, z * X + other))
            lead_swap(n, slot, when)

    def own_spread(m, carry):
        cond, copy = own_copy(m)
        pl.when(cond)(copy.wait)
        for go, out in spread(m):
            pl.when(cond & go)(out.start)
        return carry

    lax.fori_loop(0, items, own_spread, 0)

    cs_local = {}
    for k in range(STEPS):
        for b in range(B):
            src, dst = x_ref.at[k // R, b], cs_ref.at[k, b]
            for step in range(1, R):
                send(r == k % R, src, dst, cs_sem.at[k, b], (lax.rem(r + step, R), c))
            cs_local[k, b] = local(r == k % R, src, dst)

    def take(m):
        k, a, _, _, _, _ = item(m)
        return pltpu.make_async_remote_copy(
            src_ref=rs_ref.at[k, a], dst_ref=rs_ref.at[k, a], send_sem=send_sem.at[0], recv_sem=rs_sem.at[m],
            device_id=(lax.rem(r + 1, R), c), device_id_type=MESH,
        )

    skew = SKEW * jnp.maximum(z - 1, 0)
    deepest = SKEW * max(Z - 2, 0)
    per_slot = -(-items // (STEPS * GROUPS))

    def forward(s):
        m = s - skew

        @pl.when((m >= 0) & (m < items))
        def _():
            _, _, source, _, _, lane = item(m)

            @pl.when((x == lane) & (c != source))
            def _():
                take(m).wait_recv()
                for go, out in spread(m):
                    pl.when(go)(out.start)

    def slot_work(s):
        for u in range(per_slot):
            forward(s * per_slot + u)

    def lead_tile(n):
        for step in range(1, R):
            q = lax.rem(r + R - step, R)
            wait_recv(r >= 0, part(ld_ref.at[n], q), ldx_sem.at[n, step - 1])
        w_ref[n] = ld_ref[n]

    lead_tile(0)
    for k in range(STEPS):
        invert_factor(w_ref.at[SLOT[k, k]], lambda g, k=k: slot_work(k * GROUPS + g))
        inv = w_ref[SLOT[k, k]]
        if k == 0:
            for n in range(1, len(LOWER)):
                lead_tile(n)
        for i in range(k + 1, STEPS):
            w_ref[SLOT[i, k]] = dot_nt(w_ref[SLOT[i, k]], inv)
        for j in range(k + 1, STEPS):
            for i in range(j, STEPS):
                w_ref[SLOT[i, j]] = w_ref[SLOT[i, j]] - dot_nt(w_ref[SLOT[i, k]], w_ref[SLOT[j, k]])
    for k in range(STEPS):
        m_ref[SLOT[k, k]] = w_ref[SLOT[k, k]]
        for i in range(k + 1, STEPS):
            total = dot_nn(w_ref[SLOT[i, k]], m_ref[SLOT[k, k]])
            for j in range(k + 1, i):
                total = total + dot_nn(w_ref[SLOT[i, j]], m_ref[SLOT[j, k]])
            m_ref[SLOT[i, k]] = -dot_nn(w_ref[SLOT[i, i]], total)

    def late(s, carry):
        forward(s)
        return carry

    lax.fori_loop(STEPS * GROUPS * per_slot, max(items + deepest, STEPS * GROUPS * per_slot), late, 0)

    def finish_item(m, carry):
        _, _, source, _, _, lane = item(m)
        pl.when((x != lane) & (c != source))(take(m).wait_recv)
        for go, out in spread(m):
            pl.when(go)(out.wait_send)
        return carry

    lax.fori_loop(0, items, finish_item, 0)
    for k in range(STEPS):
        for b in range(B):
            pl.when(r == k % R)(cs_local[k, b])
            wait_recv(r != k % R, cs_ref.at[k, b], cs_sem.at[k, b])
    for cond, wait in pending:
        pl.when(cond)(wait)


def lead(tiles, R, C):
    A, B, T, _ = tiles.shape
    X, _ = split_col(C)
    n = len(LOWER)
    items = STEPS * A
    vmem = pl.BlockSpec(memory_space=pltpu.VMEM)
    sends = n * (R - 1) * 3 + STEPS * B * (R - 1) + n * (X + 2)
    locals_ = n + STEPS * B
    dma = pltpu.SemaphoreType.DMA
    return pl.pallas_call(
        functools.partial(lead_kernel, R, C),
        name="lead",
        out_shape=(
            jax.ShapeDtypeStruct((n, T, T), F32),
            jax.ShapeDtypeStruct((STEPS, A, T, T), F32),
            jax.ShapeDtypeStruct((STEPS, B, T, T), F32),
        ),
        in_specs=[vmem],
        out_specs=(vmem, vmem, vmem),
        scratch_shapes=[
            pltpu.VMEM((n, T, T), F32),
            pltpu.VMEM((n, T, T), F32),
            dma((sends,)), dma((locals_,)), dma((n,)), dma((n, R - 1)), dma((items,)), dma((STEPS, B)),
            dma((items, X + 2)), dma((items,)),
        ],
        compiler_params=pltpu.CompilerParams(has_side_effects=True, vmem_limit_bytes=56 * 2**20),
    )(tiles)


def halves(value):
    high = value.astype(BF16)
    return high, (value - high.astype(F32)).astype(BF16)


def dot3(p, q, dims):
    d = functools.partial(lax.dot_general, dimension_numbers=(dims, ((), ())), preferred_element_type=F32)
    return d(p[0], q[0]) + (d(p[0], q[1]) + d(p[1], q[0]))


NT = ((1,), (1,))
NN = ((1,), (0,))


def finish_kernel(R, C, x_ref, m_ref, rs_ref, cs_ref, t_ref, p_ref, mh_ref, ml_ref, qh_ref, ql_ref):
    A, B, T, _ = x_ref.shape
    r, c = lax.axis_index("row"), lax.axis_index("col")
    for n in range(len(LOWER)):
        mh_ref[n], ml_ref[n] = halves(m_ref[n])
    for b in range(B):
        terms = [halves(cs_ref[j, b]) for j in range(STEPS)]
        for k in range(STEPS):
            total = None
            for j in range(k + 1):
                n = SLOT[k, j]
                term = dot3((mh_ref[n], ml_ref[n]), terms[j], NN)
                total = term if total is None else total + term
            qh_ref[k, b], ql_ref[k, b] = halves(total)

    def body(a, carry):
        tile_row = a * R + r
        terms = [halves(rs_ref[j, a]) for j in range(STEPS)]
        panel = []
        for k in range(STEPS):
            total = None
            for j in range(k + 1):
                n = SLOT[k, j]
                term = dot3(terms[j], (mh_ref[n], ml_ref[n]), NT)
                total = term if total is None else total + term
            p_ref[a, k] = jnp.where(tile_row >= k, total, F32(0.0))
            panel.append(halves(total))
        for b in range(B):
            total = x_ref[a, b]
            for k in range(STEPS):
                total = total - dot3(panel[k], (qh_ref[k, b], ql_ref[k, b]), NN)
            keep = (tile_row >= STEPS) & (b * C + c >= STEPS)
            t_ref[a, :, b * T : (b + 1) * T] = jnp.where(keep, total, F32(0.0))
        return carry

    lax.fori_loop(0, A, body, 0)


def finish(tiles, m, rs, cs, R, C):
    A, B, T, _ = tiles.shape
    vmem = pl.BlockSpec(memory_space=pltpu.VMEM)
    n = len(LOWER)
    return pl.pallas_call(
        functools.partial(finish_kernel, R, C),
        name="finish",
        out_shape=(jax.ShapeDtypeStruct((A, T, B * T), F32), jax.ShapeDtypeStruct((A, STEPS, T, T), F32)),
        in_specs=[vmem] * 4,
        out_specs=(vmem, vmem),
        scratch_shapes=[
            pltpu.VMEM((n, T, T), BF16),
            pltpu.VMEM((n, T, T), BF16),
            pltpu.VMEM((STEPS, B, T, T), BF16),
            pltpu.VMEM((STEPS, B, T, T), BF16),
        ],
        compiler_params=pltpu.CompilerParams(vmem_limit_bytes=56 * 2**20),
    )(tiles, m, rs, cs)


def shards(kernel):
    A, _, T, B, _, _ = kernel.shape
    R, C = lax.axis_size("row"), lax.axis_size("col")
    tiles = kernel.reshape(A, T, B, T).transpose(0, 2, 1, 3)
    m, rs, cs = lead(tiles, R, C)
    trailing, panels = finish(tiles, m, rs, cs, R, C)
    return trailing.reshape(kernel.shape), panels.transpose(0, 2, 1, 3).reshape(A, 1, T, STEPS, T)


def solution(mesh):
    in_specs = (P(None, "row", None, None, "col", None),)
    out_specs = (P(None, "row", None, None, "col", None), P(None, "row", None, None, None))
    return jax.shard_map(shards, mesh=mesh, in_specs=in_specs, out_specs=out_specs, check_vma=False)
```

time: 225 us -> 124 us (0.55)
  the two profiles are of different devices: /device:TPU:28 before, /device:TPU:25 now
where the time goes in v2:
time: 124 us
  Pallas kernels  116 us (94%)
  local copies, waits for them, and re-layouts  7.81 us (6%)
    pallas_call x1, Pallas kernels, lead(): pl.pallas_call(functools.partial(lead_kernel, R, C), name='lead', out_sha...  103 us
    pallas_call x1, Pallas kernels, finish(): pl.pallas_call(functools.partial(finish_kernel, R, C), name='finish', out...  12.8 us
    reshape x1, local copies, waits for them, and re-layouts, shards(): trailing.reshape(kernel.shape)  4.7 us
    unnamed x1, local copies, waits for them, and re-layouts  3.11 us

profile of v2, /device:TPU:25, one launch (start us, length us, event | category | flops | bytes accessed | tf_op | source)
XLA Modules:
  0.0 124.0 jit_solution(73187050685958183)
XLA Ops:
  0.6 3.1 %copy.7 = f32[4,1,256,2,1,256]{5,2,3,0,4,1:T(8,128)} copy(f32[4,1,256,2,1,256]{5,4,3,2,1,0:T(1,128)} %param.1) | data formatting | bytes 4194304 | tf_op args[0]
  3.7 102.7 %lead.1 = (f32[6,256,256]{2,1,0:T(8,128)}, f32[3,4,256,256]{3,2,1,0:T(8,128)}, f32[3,2,256,256]{3,2,1,0:T(8,128)}) custom-call(f32[4,2,256,256]{3,2,1,0:T(8,128)} %bitcast.10), custom_call_target="tpu_custom_call" | custom-call | tf_op jit(solution)/shard_map/lead/pallas_call | solution.py:305
  106.5 12.8 %finish.1 = (f32[4,256,512]{2,1,0:T(8,128)}, f32[4,3,256,256]{3,2,1,0:T(8,128)}) custom-call(f32[4,2,256,256]{3,2,1,0:T(8,128)} %bitcast.11, f32[6,256,256]{2,1,0:T(8,128)} %get-tuple-element.7.m_ref, f32[3,4,256,256]{3,2,1,0:T(8,128)} %get-tuple-element.8.rs_ref, f32[3,2,256,256]{3,2,1,0:T(8,128)} %get-tuple-element.9.cs_ref), custom_call_target="tpu_custom_call" | custom-call | tf_op jit(solution)/shard_map/finish/pallas_call | solution.py:381
  119.3 4.7 %reshape.16 = f32[4,1,256,2,1,256]{5,4,3,2,1,0:T(1,128)} reshape(f32[4,256,512]{2,1,0:T(8,128)} %get-tuple-element.10) | data formatting | bytes 4194304 | tf_op jit(solution)/shard_map/reshape | solution.py:403

commit v3 on v2

--- a/solution.py
+++ b/solution.py
@@ -9,8 +9,9 @@
 
 STEPS = 3
 PANEL = 16
-GROUPS = 4
-SKEW = 2
+GROUPS = 8
+SKEW = 0
+PIECES = 2
 MESH = pl.DeviceIdType.MESH
 F32 = jnp.float32
 BF16 = jnp.bfloat16
@@ -93,7 +94,7 @@
     r, c = lax.axis_index("row"), lax.axis_index("col")
     z, x = lax.div(c, X), lax.rem(c, X)
     chunk = T // R
-    items = A * STEPS
+    items = A * STEPS * PIECES
     pending = []
     counts = {"send": 0, "local": 0}
 
@@ -133,21 +134,33 @@
         ld_local.append(local(owner, part(src, r), part(ld_ref.at[n], r)))
 
     def item(m):
-        k, a = lax.rem(m, STEPS), lax.div(m, STEPS)
+        tile, piece = lax.div(m, PIECES), lax.rem(m, PIECES)
+        rest = jnp.maximum(tile - A, 0)
+        k = jnp.where(tile < A, STEPS - 1, lax.rem(rest, STEPS - 1))
+        a = jnp.where(tile < A, tile, lax.div(rest, STEPS - 1))
         source = lax.rem(k, C)
         zs, xs = lax.div(source, X), lax.rem(source, X)
         lane = jnp.where(k < X, lax.rem(k, X), lax.rem(a, X))
-        return k, a, source, zs, xs, lane
+        return k, a, piece, source, zs, xs, lane
+
+    def need(m):
+        return item(m)[1] * R + r >= STEPS
+
+    def piece_of(m):
+        k, a, piece = item(m)[:3]
+        rows = T // PIECES
+        return rs_ref.at[k, a, pl.ds(pl.multiple_of(piece * rows, rows), rows), :]
 
     def own_copy(m):
-        k, a, source, _, _, _ = item(m)
-        copy = pltpu.make_async_copy(x_ref.at[a, lax.div(k, C)], rs_ref.at[k, a], rs_loc.at[m])
-        return c == source, copy
+        k, a, piece, source = item(m)[:4]
+        rows = T // PIECES
+        src = x_ref.at[a, lax.div(k, C), pl.ds(pl.multiple_of(piece * rows, rows), rows), :]
+        return (c == source) & need(m), pltpu.make_async_copy(src, piece_of(m), rs_loc.at[m])
 
     def spread(m):
-        k, a, source, zs, xs, lane = item(m)
-        on = x == lane
-        slot = rs_ref.at[k, a]
+        _, _, _, source, zs, xs, lane = item(m)
+        on = (x == lane) & need(m)
+        slot = piece_of(m)
 
         def copy(n, dev):
             return pltpu.make_async_remote_copy(
@@ -155,7 +168,7 @@
                 device_id=dev, device_id_type=MESH,
             )
 
-        yield (c == source) & (xs != lane), copy(0, (r, lax.rem(zs * X + lane, C)))
+        yield (c == source) & (xs != lane) & need(m), copy(0, (r, lax.rem(zs * X + lane, C)))
         yield on & (z >= zs) & (z + 1 < Z), copy(1, (r, lax.rem(c + X, C)))
         yield on & (z <= zs) & (z > 0), copy(2, (r, lax.rem(c + C - X, C)))
         for step in range(1, X):
@@ -181,24 +194,30 @@
         for step in range(1, R):
             send(when, slot, slot, ldx_sem.at[n, step - 1], (lax.rem(r + step, R), c))
 
+    def lead_pass(n, early):
+        i, j = LOWER[n]
+        lane, source = n % X, j % C
+        zs, xs = divmod(source, X)
+        on = x == lane
+        first = on | (c == source)
+        when = first if early else jnp.logical_not(first)
+        slot = lead_step(n, when)
+        if early:
+            if lane != xs:
+                send(c == source, slot, slot, ld_sem.at[n], (r, zs * X + lane))
+            send(on & (z >= zs) & (z + 1 < Z), slot, slot, ld_sem.at[n], (r, lax.rem(c + X, C)))
+            send(on & (z <= zs) & (z > 0), slot, slot, ld_sem.at[n], (r, lax.rem(c + C - X, C)))
+            for other in range(X):
+                if other != lane:
+                    cond = on & (z != zs) if other == xs else on
+                    send(cond, slot, slot, ld_sem.at[n], (r, z * X + other))
+        lead_swap(n, slot, when)
+
+    lead_pass(0, True)
+    lead_pass(0, False)
     for early in (True, False):
-        for n, (i, j) in enumerate(LOWER):
-            lane, source = n % X, j % C
-            zs, xs = divmod(source, X)
-            on = x == lane
-            first = on | (c == source)
-            when = first if early else jnp.logical_not(first)
-            slot = lead_step(n, when)
-            if early:
-                if lane != xs:
-                    send(c == source, slot, slot, ld_sem.at[n], (r, zs * X + lane))
-                send(on & (z >= zs) & (z + 1 < Z), slot, slot, ld_sem.at[n], (r, lax.rem(c + X, C)))
-                send(on & (z <= zs) & (z > 0), slot, slot, ld_sem.at[n], (r, lax.rem(c + C - X, C)))
-                for other in range(X):
-                    if other != lane:
-                        cond = on & (z != zs) if other == xs else on
-                        send(cond, slot, slot, ld_sem.at[n], (r, z * X + other))
-            lead_swap(n, slot, when)
+        for n in range(1, len(LOWER)):
+            lead_pass(n, early)
 
     def own_spread(m, carry):
         cond, copy = own_copy(m)
@@ -218,9 +237,8 @@
             cs_local[k, b] = local(r == k % R, src, dst)
 
     def take(m):
-        k, a, _, _, _, _ = item(m)
         return pltpu.make_async_remote_copy(
-            src_ref=rs_ref.at[k, a], dst_ref=rs_ref.at[k, a], send_sem=send_sem.at[0], recv_sem=rs_sem.at[m],
+            src_ref=piece_of(m), dst_ref=piece_of(m), send_sem=send_sem.at[0], recv_sem=rs_sem.at[m],
             device_id=(lax.rem(r + 1, R), c), device_id_type=MESH,
         )
 
@@ -233,9 +251,9 @@
 
         @pl.when((m >= 0) & (m < items))
         def _():
-            _, _, source, _, _, lane = item(m)
-
-            @pl.when((x == lane) & (c != source))
+            _, _, _, source, _, _, lane = item(m)
+
+            @pl.when((x == lane) & (c != source) & need(m))
             def _():
                 take(m).wait_recv()
                 for go, out in spread(m):
@@ -258,6 +276,13 @@
         if k == 0:
             for n in range(1, len(LOWER)):
                 lead_tile(n)
+            for i in range(STEPS):
+
+                @pl.when(r == i % R)
+                def _():
+                    for j in range(STEPS):
+                        rs_ref[j, i // R] = ld_ref[SLOT[i, j]] if j <= i else jnp.zeros((T, T), F32)
+
         for i in range(k + 1, STEPS):
             w_ref[SLOT[i, k]] = dot_nt(w_ref[SLOT[i, k]], inv)
         for j in range(k + 1, STEPS):
@@ -278,8 +303,8 @@
     lax.fori_loop(STEPS * GROUPS * per_slot, max(items + deepest, STEPS * GROUPS * per_slot), late, 0)
 
     def finish_item(m, carry):
-        _, _, source, _, _, lane = item(m)
-        pl.when((x != lane) & (c != source))(take(m).wait_recv)
+        _, _, _, source, _, _, lane = item(m)
+        pl.when((x != lane) & (c != source) & need(m))(take(m).wait_recv)
         for go, out in spread(m):
             pl.when(go)(out.wait_send)
         return carry
@@ -297,7 +322,7 @@
     A, B, T, _ = tiles.shape
     X, _ = split_col(C)
     n = len(LOWER)
-    items = STEPS * A
+    items = STEPS * A * PIECES
     vmem = pl.BlockSpec(memory_space=pltpu.VMEM)
     sends = n * (R - 1) * 3 + STEPS * B * (R - 1) + n * (X + 2)
     locals_ = n + STEPS * B

time: 124 us -> 112 us (0.903)
  the two profiles are of different devices: /device:TPU:25 before, /device:TPU:28 now
where the time goes in v3:
time: 112 us; the launch traced here: 111 us
  Pallas kernels  102 us (91%)
  local copies, waits for them, and re-layouts  7.81 us (7%)
    pallas_call x1, Pallas kernels, lead(): pl.pallas_call(functools.partial(lead_kernel, R, C), name='lead', out_sha...  89.6 us
    pallas_call x1, Pallas kernels, finish(): pl.pallas_call(functools.partial(finish_kernel, R, C), name='finish', out...  12.8 us
    reshape x1, local copies, waits for them, and re-layouts, shards(): trailing.reshape(kernel.shape)  4.7 us
    unnamed x1, local copies, waits for them, and re-layouts  3.11 us

profile of v3, /device:TPU:28, one launch (start us, length us, event | category | flops | bytes accessed | tf_op | source)
XLA Modules:
  0.0 110.8 jit_solution(13971141012323533137)
XLA Ops:
  0.6 3.1 %copy.7 = f32[4,1,256,2,1,256]{5,2,3,0,4,1:T(8,128)} copy(f32[4,1,256,2,1,256]{5,4,3,2,1,0:T(1,128)} %param.1) | data formatting | bytes 4194304 | tf_op args[0]
  3.7 89.6 %lead.1 = (f32[6,256,256]{2,1,0:T(8,128)}, f32[3,4,256,256]{3,2,1,0:T(8,128)}, f32[3,2,256,256]{3,2,1,0:T(8,128)}) custom-call(f32[4,2,256,256]{3,2,1,0:T(8,128)} %bitcast.10), custom_call_target="tpu_custom_call" | custom-call | tf_op jit(solution)/shard_map/lead/pallas_call | solution.py:330
  93.3 12.8 %finish.1 = (f32[4,256,512]{2,1,0:T(8,128)}, f32[4,3,256,256]{3,2,1,0:T(8,128)}) custom-call(f32[4,2,256,256]{3,2,1,0:T(8,128)} %bitcast.11, f32[6,256,256]{2,1,0:T(8,128)} %get-tuple-element.7.m_ref, f32[3,4,256,256]{3,2,1,0:T(8,128)} %get-tuple-element.8.rs_ref, f32[3,2,256,256]{3,2,1,0:T(8,128)} %get-tuple-element.9.cs_ref), custom_call_target="tpu_custom_call" | custom-call | tf_op jit(solution)/shard_map/finish/pallas_call | solution.py:406
  106.1 4.7 %reshape.16 = f32[4,1,256,2,1,256]{5,4,3,2,1,0:T(1,128)} reshape(f32[4,256,512]{2,1,0:T(8,128)} %get-tuple-element.10) | data formatting | bytes 4194304 | tf_op jit(solution)/shard_map/reshape | solution.py:428
